TPU v7x, 32 devices: a whole 2x2x4 slice. The times are simulated.
32 devices in a mesh: expert: 8 (over z, y), blk: 4 (over x, core).
Axes of the slice: x: 2, y: 2, z: 4, core: 2. Of those that a mesh axis runs over, the one named last changes fastest.
Arguments:
- inputs: bfloat16 [8, 768, 1536], P('expert', 'blk'), may hold values from -6 to 6
- output_grads: bfloat16 [8, 768, 4096], P('expert', 'blk'), may hold values from -0.21875 to 0.21875
- route_counts: int32 [8, 4], P('expert', 'blk'), may hold values from 48 to 192, as said below
- left_rows: bfloat16 [8, 2304, 1536], P(None, 'expert', 'blk'), as said below
- left_lengths: int32 [8, 8], replicated, may hold values from 96 to 288, as said below
- right_inverse: bfloat16 [8, 4096, 4096], P('expert', 'blk'), may hold values from -0.09375 to 0.09375
Outputs:
- preconditioned: float32 [8, 4096, 1536], P('expert', 'blk')
Inputs may be any that keep to these rules, and one draw needn't show every extreme that they name: `route_counts`: for every expert, one device of blk holds exactly 192 routed tokens and one holds exactly 48. `left_lengths`: each row sums to 1536; in each row one owner holds exactly 288 rows and one exactly 96. `left_rows`: slots i * 288 + j with j >= left_lengths[e, i] are zero.
All inputs are finite; a program needn't handle non-finite values.
Results may differ from a plain program's by a relative error of at most 0.0041.
Values may be sent and summed in bfloat16 or wider, within the bound.
A program may use at most 128 MiB of HBM per device.

v0:
```python
import jax
import jax.numpy as jnp
from jax import lax
from jax.sharding import PartitionSpec as P


def shards(inputs, output_grads, route_counts, left_rows, left_lengths, right_inverse):
    token_rows = inputs[0]
    slot_count, width_in = token_rows.shape
    owners, piece_slots = (left_lengths.shape[1], left_rows.shape[1])
    live_rows = lax.broadcasted_iota(jnp.int32, (slot_count, 1), 0) < route_counts[0, 0]
    masked = jnp.where(live_rows, token_rows, jnp.zeros_like(token_rows))
    tokens = lax.all_gather(masked, "blk", axis=0, tiled=True)
    grads = lax.all_gather(output_grads[0], "blk", axis=0, tiled=True)
    arrived = lax.all_to_all(left_rows, "expert", split_axis=0, concat_axis=1, tiled=True)[0]
    lengths = lax.dynamic_index_in_dim(left_lengths, lax.axis_index("expert"), 0, keepdims=False)
    starts = jnp.cumsum(lengths) - lengths
    offset = lax.broadcasted_iota(jnp.int32, (owners, piece_slots), 1)
    row_index = jnp.where(offset < lengths[:, None], starts[:, None] + offset, -1)
    row_index = row_index.reshape(1, owners * piece_slots)
    select = lax.broadcasted_iota(jnp.int32, (width_in, 1), 0) == row_index
    picked = jnp.dot(tokens, select.astype(jnp.bfloat16), preferred_element_type=jnp.float32)
    picked = picked.astype(jnp.bfloat16)
    mixed = lax.dot_general(
        arrived, picked, (((0,), (1,)), ((), ())), preferred_element_type=jnp.float32
    ).astype(jnp.bfloat16)
    mixed = lax.all_gather(mixed, "blk", axis=0, tiled=True)
    trans_b = (((1,), (1,)), ((), ()))
    scores = lax.dot_general(
        right_inverse[0], grads, trans_b, preferred_element_type=jnp.float32
    ).astype(jnp.bfloat16)
    result = lax.dot_general(scores, mixed, trans_b, preferred_element_type=jnp.float32)
    return result[None]


def solution(mesh):
    in_specs = (
        P("expert", "blk", None),
        P("expert", "blk", None),
        P("expert", "blk"),
        P(None, "expert", "blk"),
        P(),
        P("expert", "blk", None),
    )
    out_specs = P("expert", "blk", None)
    return jax.shard_map(shards, mesh=mesh, in_specs=in_specs, out_specs=out_specs, check_vma=False)
```

profile of v0, /device:TPU:0, one launch (start us, length us, event | category | flops | bytes accessed | tf_op | source)
XLA Modules:
  0.0 165.5 jit_solution(11271811725548098723)
XLA Ops:
  6.5 0.0 all-gather.5.cloned.1.call-start
  7.2 2.0 %bitcast_select_fusion = bf16[192,1536]{1,0:T(8,128)(2,1)} fusion(bf16[1,192,1536]{2,1,0:T(8,128)(2,1)} %param.6, pred[192]{0:T(512)(128)(4,1)S(1)} %iota_compare_fusion.7), kind=kLoop, calls=%fused_computation.11 | loop fusion | flops 294912 | bytes 1179840 | tf_op jit(solution)/shard_map/jit(_where)/select_n | solution.py:12
  9.2 0.0 all-gather.5.cloned.1.call-update
  9.2 7.3 %all-to-all-start = ((bf16[8,288,384]{2,1,0:T(8,128)(2,1)}), bf16[8,288,384]{2,1,0:T(8,128)(2,1)S(1)}, u32[]{:S(2)}, u32[]{:S(2)}) async-start(bf16[8,288,384]{2,1,0:T(8,128)(2,1)} %param.9), calls=%async_computation | async-start | bytes 3538944 | tf_op jit(solution)/shard_map/all_to_all | solution.py:15
  16.5 0.0 all-gather.7.cloned.1.call-start
  16.6 0.7 fusion.16
  17.3 0.2 reduce-window.8
  17.5 0.7 bitcast_subtract_fusion
  18.2 0.1 add_select_fusion
  18.2 0.1 select_n.22
  18.3 39.4 %all-to-all-done = bf16[8,288,384]{2,1,0:T(8,128)(2,1)S(1)} async-done(((bf16[8,288,384]{2,1,0:T(8,128)(2,1)}), bf16[8,288,384]{2,1,0:T(8,128)(2,1)S(1)}, u32[]{:S(2)}, u32[]{:S(2)}) %all-to-all-start) | async-done | bytes 1769504 | tf_op jit(solution)/shard_map/all_to_all | solution.py:15
  57.8 0.0 all-gather.5.cloned.1.call-done
  57.8 10.0 %fusion.15 = bf16[384,768]{0,1:T(8,128)(2,1)} fusion(bf16[2304,384]{1,0:T(8,128)(2,1)S(1)} %bitcast.33, bf16[768,1536]{1,0:T(8,128)(2,1)} %all-gather.5.cloned.1.call-done, s32[2304]{0:T(1024)S(1)} %select_n.22), kind=kOutput, calls=%fused_computation.10 | convolution fusion | flops 6800375808 | bytes 4727808 | tf_op jit(solution)/shard_map/dot_general | solution.py:24
  67.8 0.0 all-gather.7.cloned.1.call-update
  67.8 0.0 all-gather.9.cloned.1.call-start
  67.8 0.7 all-gather.9.cloned.1.call-update
  68.5 22.5 %all-gather.7.cloned.1.call-done = bf16[1536,768]{0,1:T(8,128)(2,1)} async-done(((bf16[384,768]{0,1:T(8,128)(2,1)}), bf16[1536,768]{0,1:T(8,128)(2,1)}) %all-gather.7.cloned.1.call-update) | async-done | bytes 2359312 | tf_op jit(solution)/shard_map/all_gather | solution.py:27
  91.0 48.0 %all-gather.9.cloned.1.call-done = bf16[1,768,4096]{2,1,0:T(8,128)(2,1)} async-done(((bf16[1,192,4096]{2,1,0:T(8,128)(2,1)}), bf16[1,768,4096]{2,1,0:T(8,128)(2,1)}) %all-gather.9.cloned.1.call-update) | async-done | bytes 6291472 | tf_op jit(solution)/shard_map/all_gather | solution.py:14
  139.0 20.0 %convolution_bitcast_fusion = f32[1,1024,1536]{2,1,0:T(8,128)} fusion(bf16[1536,768]{0,1:T(8,128)(2,1)} %all-gather.7.cloned.1.call-done, bf16[1,768,4096]{2,1,0:T(8,128)(2,1)} %all-gather.9.cloned.1.call-done, bf16[1,1024,4096]{2,1,0:T(8,128)(2,1)} %param.11), kind=kOutput, calls=%fused_computation.7 | convolution fusion | flops 8859156480 | bytes 23330816 | tf_op jit(solution)/shard_map/dot_general | solution.py:32
  (1 shorter events, 0.0 us)
Async XLA Ops:
  6.5 51.2 %all-gather.5.cloned.1.call-start = ((), (), s32[]{:S(2)}) async-start(), calls=%async_computation.1 | async-start | bytes 2949120 | tf_op jit(solution)/shard_map/all_gather | solution.py:13
  9.2 48.5 %all-to-all-start = ((bf16[8,288,384]{2,1,0:T(8,128)(2,1)}), bf16[8,288,384]{2,1,0:T(8,128)(2,1)S(1)}, u32[]{:S(2)}, u32[]{:S(2)}) async-start(bf16[8,288,384]{2,1,0:T(8,128)(2,1)} %param.9), calls=%async_computation | async-start | bytes 3538944 | tf_op jit(solution)/shard_map/all_to_all | solution.py:15
  16.5 74.5 %all-gather.7.cloned.1.call-start = ((), (), s32[]{:S(2)}) async-start(), calls=%async_computation.2 | async-start | bytes 2949120 | tf_op jit(solution)/shard_map/all_gather | solution.py:27
  67.8 71.2 %all-gather.9.cloned.1.call-start = ((), (), s32[]{:S(2)}) async-start(), calls=%async_computation.3 | async-start | bytes 7864320 | tf_op jit(solution)/shard_map/all_gather | solution.py:14
Sparse Core Ops, SparseCore 0:
  9.3 26.7 all-gather.4
  67.9 23.0 all-gather.6
  92.6 46.3 all-gather.8
where the time goes:
time: 166 us
  waiting for transfers between devices  111 us (67%)
  matrix products  30 us (18%)
  between operations  13.8 us (8%)
  starting transfers between devices  7.4 us (4%)
  other arithmetic  2.95 us (2%)
    all_gather x1, waiting for transfers between devices, shards(): grads = lax.all_gather(output_grads[0], 'blk', axis=0, tiled=True)  48 us
    all_to_all x1, waiting for transfers between devices, shards(): lax.all_to_all(left_rows, 'expert', split_axis=0, concat_axis=1, tiled=True)  39.4 us
    all_gather x1, waiting for transfers between devices, shards(): mixed = lax.all_gather(mixed, 'blk', axis=0, tiled=True)  22.5 us
    dot_general x1, matrix products, shards(): lax.dot_general(scores, mixed, trans_b, preferred_element_type=jnp.float32)  20 us
    dot_general x1, matrix products, shards(): lax.dot_general(arrived, picked, (((0,), (1,)), ((), ())), preferred_elem...  10 us
    all_to_all x1, starting transfers between devices, shards(): lax.all_to_all(left_rows, 'expert', split_axis=0, concat_axis=1, tiled=True)  7.32 us
  transfers between devices with their start and end apart: 4, of which 3 were waited for; matrix products, arithmetic and copies ran while one was open for 1% of the time, Pallas kernels for 0%

commit v1 on v0

--- a/solution.py
+++ b/solution.py
@@ -2,6 +2,35 @@
 import jax.numpy as jnp
 from jax import lax
 from jax.sharding import PartitionSpec as P
+
+
+def links_recast(view, row_dim):
+    view = jnp.moveaxis(view, 0, row_dim)
+    found_now = view.shape
+    return view.reshape(
+        *found_now[:row_dim], found_now[row_dim] * found_now[row_dim + 1], *found_now[row_dim + 2 :]
+    )
+
+
+def measure_chunk(mine_x, row_axis):
+    next_value = lax.axis_size(row_axis)
+    b_next = lax.axis_index(row_axis)
+    view_out, piece_out = (next_value, b_next)
+    val, taken_in = (mine_x[None], 1)
+    while taken_in < view_out:
+        long_array = lax.ppermute(
+            val, row_axis, [(dev_i, dev_i ^ taken_in) for dev_i in range(view_out)]
+        )
+        local_next = piece_out & taken_in == 0
+        val = jnp.concatenate(
+            [jnp.where(local_next, val, long_array), jnp.where(local_next, long_array, val)]
+        )
+        taken_in *= 2
+    return val
+
+
+def change_surface(panel, base_x, d_out):
+    return links_recast(measure_chunk(panel, base_x), d_out)
 
 
 def shards(inputs, output_grads, route_counts, left_rows, left_lengths, right_inverse):
@@ -11,7 +40,7 @@
     live_rows = lax.broadcasted_iota(jnp.int32, (slot_count, 1), 0) < route_counts[0, 0]
     masked = jnp.where(live_rows, token_rows, jnp.zeros_like(token_rows))
     tokens = lax.all_gather(masked, "blk", axis=0, tiled=True)
-    grads = lax.all_gather(output_grads[0], "blk", axis=0, tiled=True)
+    grads = change_surface(output_grads[0], base_x="blk", d_out=0)
     arrived = lax.all_to_all(left_rows, "expert", split_axis=0, concat_axis=1, tiled=True)[0]
     lengths = lax.dynamic_index_in_dim(left_lengths, lax.axis_index("expert"), 0, keepdims=False)
     starts = jnp.cumsum(lengths) - lengths

time: 166 us -> 143 us (0.86)
  waiting for transfers between devices: 111 us -> 80 us
  other arithmetic: 2.95 us -> 12.5 us
  matrix products: 30 us -> 26.5 us
    all_gather x1 -> x0, waiting for transfers between devices: 48 us -> none  [shards(): grads = lax.all_gather(output_grads[0], 'blk', axis=0, tiled=True)]
    ppermute x0 -> x2, waiting for transfers between devices: none -> 45.5 us  [measure_chunk(): lax.ppermute(val, row_axis, [(dev_i, dev_i ^ taken_in) for dev_i in range...]
    all_gather x1, waiting for transfers between devices: 22.5 us -> 0.01 us  [shards(): mixed = lax.all_gather(mixed, 'blk', axis=0, tiled=True)]
    concatenate x0 -> x2, other arithmetic: none -> 5.14 us  [measure_chunk(): jnp.concatenate([jnp.where(local_next, val, long_array), jnp.where(local_...]
    all_to_all x1, waiting for transfers between devices: 39.4 us -> 34.4 us  [shards(): lax.all_to_all(left_rows, 'expert', split_axis=0, concat_axis=1, tiled=True)]
    select_n x0 -> x2, other arithmetic: none -> 4.45 us  [measure_chunk(): jnp.where(local_next, val, long_array)]
    dot_general x1, matrix products: 20 us -> 15.9 us  [shards(): lax.dot_general(scores, mixed, trans_b, preferred_element_type=jnp.float32)]
    ppermute x0 -> x2, starting transfers between devices: none -> 2.04 us  [measure_chunk(): lax.ppermute(val, row_axis, [(dev_i, dev_i ^ taken_in) for dev_i in range...]
  transfers between devices with their start and end apart: 4 -> 5, of which waited for: 3 -> 2; matrix products, arithmetic and copies ran while one was open for 1% -> 15% of each run, Pallas kernels for 0% -> 0%
where the time goes in v1:
time: 143 us
  waiting for transfers between devices  80 us (56%)
  matrix products  26.5 us (19%)
  between operations  14.1 us (10%)
  other arithmetic  12.5 us (9%)
  starting transfers between devices  8.93 us (6%)
    ppermute x2, waiting for transfers between devices, measure_chunk(): lax.ppermute(val, row_axis, [(dev_i, dev_i ^ taken_in) for dev_i in range...  45.5 us
    all_to_all x1, waiting for transfers between devices, shards(): lax.all_to_all(left_rows, 'expert', split_axis=0, concat_axis=1, tiled=True)  34.4 us
    dot_general x1, matrix products, shards(): lax.dot_general(scores, mixed, trans_b, preferred_element_type=jnp.float32)  15.9 us
    dot_general x1, matrix products, shards(): lax.dot_general(arrived, picked, (((0,), (1,)), ((), ())), preferred_elem...  10.6 us
    all_to_all x1, starting transfers between devices, shards(): lax.all_to_all(left_rows, 'expert', split_axis=0, concat_axis=1, tiled=True)  6.85 us
    concatenate x2, other arithmetic, measure_chunk(): jnp.concatenate([jnp.where(local_next, val, long_array), jnp.where(local_...  5.14 us
    select_n x2, other arithmetic, measure_chunk(): jnp.where(local_next, val, long_array)  4.45 us
  transfers between devices with their start and end apart: 5, of which 2 were waited for; matrix products, arithmetic and copies ran while one was open for 15% of the time, Pallas kernels for 0%

profile of v1, /device:TPU:0, one launch (start us, length us, event | category | flops | bytes accessed | tf_op | source)
XLA Modules:
  0.0 142.8 jit_solution(7676264290474321004)
XLA Ops:
  6.5 0.0 all-gather.3.cloned.1.call-start
  7.2 2.0 %bitcast_select_fusion = bf16[192,1536]{1,0:T(8,128)(2,1)} fusion(bf16[1,192,1536]{2,1,0:T(8,128)(2,1)} %param.6, pred[192]{0:T(512)(128)(4,1)S(1)} %iota_compare_fusion.7), kind=kLoop, calls=%fused_computation.16 | loop fusion | flops 294912 | bytes 1179840 | tf_op jit(solution)/shard_map/jit(_where)/select_n | solution.py:41
  9.2 0.0 all-gather.3.cloned.1.call-update
  9.2 0.6 collective-permute-start
  9.8 6.8 %all-to-all-start = ((bf16[8,288,384]{2,1,0:T(8,128)(2,1)}), bf16[8,288,384]{2,1,0:T(8,128)(2,1)}, u32[]{:S(2)}, u32[]{:S(2)}) async-start(bf16[8,288,384]{2,1,0:T(8,128)(2,1)} %param.9), calls=%async_computation | async-start | bytes 3538944 | tf_op jit(solution)/shard_map/all_to_all | solution.py:44
  16.6 0.0 all-gather.5.cloned.1.call-start
  16.7 0.7 fusion.11
  17.4 0.2 reduce-window.8
  17.6 0.7 bitcast_subtract_fusion
  18.3 0.1 add_select_fusion
  18.3 0.1 select_n.52
  18.4 0.0 collective-permute-done
  18.4 2.3 %broadcast_select_fusion.3 = (bf16[1,192,4096]{2,1,0:T(8,128)(2,1)S(1)}, bf16[1,192,4096]{2,1,0:T(8,128)(2,1)S(1)}) fusion(bf16[1,192,4096]{2,1,0:T(8,128)(2,1)} %param.7, bf16[1,192,4096]{2,1,0:T(8,128)(2,1)} %collective-permute-done, pred[]{:T(512)S(6)} %eq.20), kind=kLoop, calls=%fused_computation.13 | loop fusion | flops 1572864 | bytes 6291457 | tf_op jit(solution)/shard_map/jit(_where)/select_n | solution.py:26
  20.8 1.9 %pad_maximum_fusion.1 = bf16[2,192,4096]{2,1,0:T(8,128)(2,1)} fusion(bf16[1,192,4096]{2,1,0:T(8,128)(2,1)S(1)} %get-tuple-element.10, bf16[1,192,4096]{2,1,0:T(8,128)(2,1)S(1)} %get-tuple-element.9), kind=kLoop, calls=%fused_computation.8 | loop fusion | flops 1572864 | bytes 6291456 | tf_op jit(solution)/shard_map/concatenate | solution.py:25
  22.7 1.5 %collective-permute-start.1 = (bf16[2,192,4096]{2,1,0:T(8,128)(2,1)}, bf16[2,192,4096]{2,1,0:T(8,128)(2,1)}, u32[]{:S(2)}, u32[]{:S(2)}) collective-permute-start(bf16[2,192,4096]{2,1,0:T(8,128)(2,1)} %pad_maximum_fusion.1), channel_id=1, source_target_pairs={{0,2},{1,3},{2,0},{3,1},{4,6},{5,7},{6,4},{7,5},{8,10},{9,11},{10,... | collective-permute-start | bytes 9437192 | tf_op jit(solution)/shard_map/ppermute | solution.py:21
  24.2 34.4 %all-to-all-done = bf16[8,288,384]{2,1,0:T(8,128)(2,1)} async-done(((bf16[8,288,384]{2,1,0:T(8,128)(2,1)}), bf16[8,288,384]{2,1,0:T(8,128)(2,1)}, u32[]{:S(2)}, u32[]{:S(2)}) %all-to-all-start) | async-done | bytes 1769504 | tf_op jit(solution)/shard_map/all_to_all | solution.py:44
  58.6 0.0 all-gather.3.cloned.1.call-done
  58.6 10.6 %fusion.8 = bf16[384,768]{0,1:T(8,128)(2,1)} fusion(bf16[2304,384]{1,0:T(8,128)(2,1)} %bitcast.7, bf16[768,1536]{1,0:T(8,128)(2,1)} %all-gather.3.cloned.1.call-done, s32[2304]{0:T(1024)S(1)} %select_n.52), kind=kOutput, calls=%fused_computation.15 | convolution fusion | flops 6800375808 | bytes 4727808 | tf_op jit(solution)/shard_map/dot_general | solution.py:53
  69.2 0.0 all-gather.5.cloned.1.call-update
  69.3 45.5 %collective-permute-done.1 = bf16[2,192,4096]{2,1,0:T(8,128)(2,1)} collective-permute-done((bf16[2,192,4096]{2,1,0:T(8,128)(2,1)}, bf16[2,192,4096]{2,1,0:T(8,128)(2,1)}, u32[]{:S(2)}, u32[]{:S(2)}) %collective-permute-start.1) | collective-permute-done | bytes 3145760 | tf_op jit(solution)/shard_map/ppermute | solution.py:21
  114.8 2.1 %broadcast_select_fusion.1 = (bf16[2,192,4096]{2,1,0:T(8,128)(2,1)S(1)}, bf16[2,192,4096]{2,1,0:T(8,128)(2,1)S(1)}) fusion(bf16[2,192,4096]{2,1,0:T(8,128)(2,1)} %collective-permute-done.1, pred[]{:T(512)S(6)} %eq.19, bf16[1,192,4096]{2,1,0:T(8,128)(2,1)S(1)} %get-tuple-element.10, bf16[1,192,4096]{2,1,0:T(8,128)(2,1)S(1)} %get-tuple-element.9), kind=kLoop, calls=%fused_computation.10 | loop fusion | flops 4718592 | bytes 12582913 | tf_op jit(solution)/shard_map/jit(_where)/select_n | solution.py:26
  116.9 3.2 %pad_maximum_fusion = bf16[4,192,4096]{2,1,0:T(8,128)(2,1)} fusion(bf16[2,192,4096]{2,1,0:T(8,128)(2,1)S(1)} %get-tuple-element.8, bf16[2,192,4096]{2,1,0:T(8,128)(2,1)S(1)} %get-tuple-element.7), kind=kLoop, calls=%fused_computation.5 | loop fusion | flops 3145728 | bytes 12582912 | tf_op jit(solution)/shard_map/concatenate | solution.py:25
  120.1 0.0 all-gather.5.cloned.1.call-done
  120.1 15.9 %convolution_bitcast_fusion = f32[1,1024,1536]{2,1,0:T(8,128)} fusion(bf16[1536,768]{0,1:T(8,128)(2,1)} %all-gather.5.cloned.1.call-done, bf16[768,4096]{1,0:T(8,128)(2,1)} %bitcast.28, bf16[1,1024,4096]{2,1,0:T(8,128)(2,1)} %param.11), kind=kOutput, calls=%fused_computation.7 | convolution fusion | flops 8859156480 | bytes 23330816 | tf_op jit(solution)/shard_map/dot_general | solution.py:61
  (1 shorter events, 0.0 us)
Async XLA Ops:
  6.5 52.1 %all-gather.3.cloned.1.call-start = ((), (), s32[]{:S(2)}) async-start(), calls=%async_computation.1 | async-start | bytes 2949120 | tf_op jit(solution)/shard_map/all_gather | solution.py:42
  9.2 9.2 %collective-permute-start = (bf16[1,192,4096]{2,1,0:T(8,128)(2,1)}, bf16[1,192,4096]{2,1,0:T(8,128)(2,1)}, u32[]{:S(2)}, u32[]{:S(2)}) collective-permute-start(bf16[1,192,4096]{2,1,0:T(8,128)(2,1)} %param.7), channel_id=1, source_target_pairs={{0,1},{1,0},{2,3},{3,2},{4,5},{5,4},{6,7},{7,6},{8,9},{9,8},{10,11... | collective-permute-start | bytes 4718600 | tf_op jit(solution)/shard_map/ppermute | solution.py:21
  9.8 48.8 %all-to-all-start = ((bf16[8,288,384]{2,1,0:T(8,128)(2,1)}), bf16[8,288,384]{2,1,0:T(8,128)(2,1)}, u32[]{:S(2)}, u32[]{:S(2)}) async-start(bf16[8,288,384]{2,1,0:T(8,128)(2,1)} %param.9), calls=%async_computation | async-start | bytes 3538944 | tf_op jit(solution)/shard_map/all_to_all | solution.py:44
  16.6 103.5 %all-gather.5.cloned.1.call-start = ((), (), s32[]{:S(2)}) async-start(), calls=%async_computation.2 | async-start | bytes 2949120 | tf_op jit(solution)/shard_map/all_gather | solution.py:56
  22.7 92.1 %collective-permute-start.1 = (bf16[2,192,4096]{2,1,0:T(8,128)(2,1)}, bf16[2,192,4096]{2,1,0:T(8,128)(2,1)}, u32[]{:S(2)}, u32[]{:S(2)}) collective-permute-start(bf16[2,192,4096]{2,1,0:T(8,128)(2,1)} %pad_maximum_fusion.1), channel_id=1, source_target_pairs={{0,2},{1,3},{2,0},{3,1},{4,6},{5,7},{6,4},{7,5},{8,10},{9,11},{10,... | collective-permute-start | bytes 9437192 | tf_op jit(solution)/shard_map/ppermute | solution.py:21
Sparse Core Ops, SparseCore 0:
  9.3 35.6 all-gather.2
  69.4 35.7 all-gather.4
